TPU v7x, 32 devices: a whole 2x2x4 slice. The times are simulated.
32 devices in a mesh: ctx: 8 (over y, x, core), exp: 4 (over z).
Axes of the slice: x: 2, y: 2, z: 4, core: 2. Of those that a mesh axis runs over, the one named last changes fastest.
Arguments:
- tokens: bfloat16 [4096, 2048], P(('ctx', 'exp')), may hold values from -6 to 6
- cotangent: bfloat16 [4096, 2048], P(('ctx', 'exp')), may hold values from -6 to 6
- expert_ids: int32 [4096, 1], P(('ctx', 'exp')), may hold values from 0 to 3; in each aligned block of 128 rows (0 to 127, 128 to 255, ...) at most 48 rows name the same one
- route_weights: float32 [4096, 1], P(('ctx', 'exp')), may hold values from 0.1 to 1
- w_gate: bfloat16 [4, 2048, 768], P('exp', 'ctx'), may hold values from -0.125 to 0.125
- w_up: bfloat16 [4, 2048, 768], P('exp', 'ctx'), may hold values from -0.125 to 0.125
- w_down: bfloat16 [4, 768, 2048], P('exp', None, 'ctx'), may hold values from -0.21875 to 0.21875
Outputs:
- token_grads: bfloat16 [4096, 2048], P(('ctx', 'exp'))
- route_grads: float32 [4096, 1], P(('ctx', 'exp'))
- gate_grads: bfloat16 [4, 2048, 768], P('exp', 'ctx')
- up_grads: bfloat16 [4, 2048, 768], P('exp', 'ctx')
- down_grads: bfloat16 [4, 768, 2048], P('exp', None, 'ctx')
Inputs may be any that keep to these rules, and one draw needn't show every extreme that they name: `expert_ids`: among the 128 routes of one device's tokens no expert is named more than 48 times, a bound that some block reaches; the routes of one token name different experts.
All inputs are finite; a program needn't handle non-finite values.
Results may differ from a plain program's by a relative error of at most 0.018.
Values may be sent and summed in bfloat16 or wider, within the bound.
A program may use at most 64 MiB of HBM per device.

v0:
```python
import jax
import jax.numpy as jnp
from jax import lax
from jax.sharding import PartitionSpec as P


def slot_table(route_ids, expert_count, capacity):
    labels = jnp.arange(expert_count, dtype=jnp.int32)
    onehot = (route_ids[..., :, None] == labels).astype(jnp.int32)
    position = jnp.sum((jnp.cumsum(onehot, axis=-2) - 1) * onehot, axis=-1)
    target = route_ids * capacity + position
    places = jnp.arange(expert_count * capacity, dtype=jnp.int32)
    return (target[..., None, :] == places[:, None]).astype(jnp.bfloat16)


def forward_hidden(totals, units):
    gate_pre = totals[:, :units]
    up_pre = totals[:, units:]
    gate_sig = jax.nn.sigmoid(gate_pre)
    return (gate_pre * gate_sig * up_pre).astype(jnp.bfloat16)


def backward_grads(totals, back_sum, units):
    gate_pre = totals[:, :units]
    up_pre = totals[:, units:]
    gate_sig = jax.nn.sigmoid(gate_pre)
    d_up = (back_sum * gate_pre * gate_sig).astype(jnp.bfloat16)
    d_gate = (back_sum * up_pre * gate_sig * (1.0 + gate_pre * (1.0 - gate_sig))).astype(
        jnp.bfloat16
    )
    return jnp.concatenate([d_gate, d_up], axis=1)


def body(tokens, cotangent, expert_ids, route_weights, w_gate, w_up, w_down):
    ctx_size = lax.axis_size("ctx")
    exp_size = lax.axis_size("exp")
    tok_count, model_width = tokens.shape
    route_count = expert_ids.shape[1]
    slot_count = tok_count * route_count
    expert_count = w_gate.shape[0] * exp_size
    capacity = max(2, (3 * slot_count + 2 * expert_count - 1) // (2 * expert_count))
    col_count = model_width // ctx_size
    units = w_gate.shape[2]
    row_count = ctx_size * exp_size * capacity
    own_rows = row_count // ctx_size
    all_ids = lax.all_gather(expert_ids, "ctx", axis=0, tiled=True)
    tables = slot_table(all_ids.reshape(ctx_size, slot_count), expert_count, capacity)
    token_slots = jnp.repeat(tokens, route_count, axis=0)
    scaled = (
        route_weights * jnp.repeat(cotangent, route_count, axis=0).astype(jnp.float32)
    ).astype(jnp.bfloat16)
    own_table = lax.dynamic_index_in_dim(tables, lax.axis_index("ctx"), 0, keepdims=False)
    send_x = jnp.dot(own_table, token_slots, preferred_element_type=jnp.float32).astype(
        jnp.bfloat16
    )
    send_y = jnp.dot(own_table, scaled, preferred_element_type=jnp.float32).astype(jnp.bfloat16)
    send_x = send_x.reshape(expert_count, capacity, model_width)
    send_y = send_y.reshape(expert_count, capacity, model_width)
    group_x, group_y = (
        lax.all_to_all(send_x, "exp", split_axis=0, concat_axis=0, tiled=True),
        lax.all_to_all(send_y, "exp", split_axis=0, concat_axis=0, tiled=True),
    )
    slot_x, slot_y = (
        lax.all_to_all(group_x, "ctx", split_axis=2, concat_axis=0, tiled=True),
        lax.all_to_all(group_y, "ctx", split_axis=2, concat_axis=0, tiled=True),
    )
    slot_x = slot_x.reshape(row_count, col_count)
    slot_y = slot_y.reshape(row_count, col_count)
    gate_weight = w_gate[0]
    up_weight = w_up[0]
    down_weight = w_down[0]
    both_weights = jnp.concatenate([gate_weight, up_weight], axis=1)

    def fold_grad(segment):
        gate_acc = lax.dot_general(
            slot_x, segment[:, :units], (((0,), (0,)), ((), ())), preferred_element_type=jnp.float32
        )
        up_acc = lax.dot_general(
            slot_x, segment[:, units:], (((0,), (0,)), ((), ())), preferred_element_type=jnp.float32
        )
        grad_rows = lax.dot_general(
            segment, both_weights, (((1,), (1,)), ((), ())), preferred_element_type=jnp.float32
        )
        return (gate_acc, up_acc, grad_rows)

    row_x, row_y = (
        lax.all_to_all(slot_x, "ctx", split_axis=0, concat_axis=1, tiled=True),
        lax.all_to_all(slot_y, "ctx", split_axis=0, concat_axis=1, tiled=True),
    )
    full_gate, full_up, full_down = (
        lax.all_gather(gate_weight, "ctx", axis=0, tiled=True),
        lax.all_gather(up_weight, "ctx", axis=0, tiled=True),
        lax.all_gather(down_weight, "ctx", axis=1, tiled=True),
    )
    full_both = jnp.concatenate([full_gate, full_up], axis=1).reshape(
        ctx_size, col_count, 2 * units
    )
    gate_blocks = jnp.einsum(
        "rcd,cdf->crf",
        row_x.reshape(own_rows, ctx_size, col_count),
        full_both,
        preferred_element_type=jnp.float32,
    ).astype(jnp.bfloat16)
    totals_own = jnp.sum(gate_blocks.astype(jnp.float32), axis=0)
    hidden_own = forward_hidden(totals_own, units)
    back_blocks = jnp.einsum(
        "rcd,fcd->crf",
        row_y.reshape(own_rows, ctx_size, col_count),
        full_down.reshape(units, ctx_size, col_count),
        preferred_element_type=jnp.float32,
    ).astype(jnp.bfloat16)
    back_own = jnp.sum(back_blocks.astype(jnp.float32), axis=0)
    grads_own = backward_grads(totals_own, back_own, units)
    segment = (
        lax.all_gather(hidden_own, "ctx", axis=0, tiled=True),
        lax.all_gather(grads_own, "ctx", axis=0, tiled=True),
    )
    fold_segment = segment[0]
    outputs = jnp.dot(fold_segment, down_weight, preferred_element_type=jnp.float32)
    inner_rows = jnp.sum(slot_y.astype(jnp.float32) * outputs, axis=1)
    inner_all = inner_rows
    down_acc = lax.dot_general(
        fold_segment, slot_y, (((0,), (0,)), ((), ())), preferred_element_type=jnp.float32
    )
    down_state = (down_acc, inner_all)
    grad_state = fold_grad(segment[1])
    down_acc = down_state[0]
    inner_all = down_state[1]
    gate_acc = grad_state[0]
    up_acc = grad_state[1]
    back_rows = grad_state[2]
    back_slots = back_rows.astype(jnp.bfloat16).reshape(ctx_size, exp_size, capacity, col_count)
    inner_slots = inner_all.reshape(ctx_size, exp_size, capacity)
    home_back = lax.all_to_all(back_slots, "exp", split_axis=1, concat_axis=1, tiled=True)
    home_inner = lax.all_to_all(inner_slots, "exp", split_axis=1, concat_axis=1, tiled=True)
    merged = jnp.einsum(
        "cks,ckd->csd",
        tables,
        home_back.reshape(ctx_size, expert_count * capacity, col_count),
        preferred_element_type=jnp.float32,
    )
    merged = jnp.sum(merged.reshape(ctx_size, tok_count, route_count, col_count), axis=2).astype(
        jnp.bfloat16
    )
    grads_home = lax.all_to_all(merged, "ctx", split_axis=0, concat_axis=2, tiled=True)
    token_grads = grads_home.reshape(tok_count, model_width)
    inner_home = jnp.einsum(
        "cks,ck->cs",
        tables.astype(jnp.float32),
        home_inner.reshape(ctx_size, expert_count * capacity),
        precision=lax.Precision.HIGHEST,
    )
    route_sums = lax.psum_scatter(inner_home, "ctx", scatter_dimension=0, tiled=True).reshape(
        tok_count, route_count
    )
    route_grads = route_sums / route_weights
    gate_grads = gate_acc.astype(jnp.bfloat16)[None]
    up_grads = up_acc.astype(jnp.bfloat16)[None]
    down_grads = down_acc.astype(jnp.bfloat16)[None]
    return (token_grads, route_grads, gate_grads, up_grads, down_grads)


def solution(mesh):
    return jax.shard_map(
        body,
        mesh=mesh,
        in_specs=(
            P(("ctx", "exp"), None),
            P(("ctx", "exp"), None),
            P(("ctx", "exp"), None),
            P(("ctx", "exp"), None),
            P("exp", "ctx", None),
            P("exp", "ctx", None),
            P("exp", None, "ctx"),
        ),
        out_specs=(
            P(("ctx", "exp"), None),
            P(("ctx", "exp"), None),
            P("exp", "ctx", None),
            P("exp", "ctx", None),
            P("exp", None, "ctx"),
        ),
        check_vma=False,
    )
```

profile of v0, /device:TPU:0, one launch (start us, length us, event | category | flops | bytes accessed | tf_op | source)
XLA Modules:
  0.0 269.7 jit_solution(1433237262053152039)
XLA Ops:
  7.2 2.0 copy.87
  9.3 0.7 all-gather.15.cloned.1.call-update
  10.0 0.7 all-gather.17.cloned.1.call-update
  10.7 10.3 %all_gather.18 = s32[1024,1]{0,1:T(1,128)S(1)} all-gather(s32[128,1]{0,1:T(1,128)} %param.9), channel_id=1, replica_groups=mesh['ctx'=8,'exp'=4] {'ctx'}, dimensions={0}, use_global_device_ids=true | all-gather | bytes 4608 | tf_op jit(solution)/shard_map/all_gather | solution.py:46
  21.0 0.1 copy.82
  21.1 2.5 select_reduce_fusion
  23.7 0.1 iota_compare_fusion
  23.8 2.4 convolution_convert_fusion.2
  26.2 4.9 %all-to-all-start = ((bf16[4,48,2048]{2,1,0:T(8,128)(2,1)}), bf16[4,48,2048]{2,1,0:T(8,128)(2,1)S(1)}, u32[]{:S(2)}, u32[]{:S(2)}) async-start(bf16[4,48,2048]{2,1,0:T(8,128)(2,1)} %bitcast.3), calls=%async_computation | async-start | bytes 1572864 | tf_op jit(solution)/shard_map/all_to_all | solution.py:61
  31.1 1.3 convolution_convert_fusion.1
  32.4 19.3 %all-to-all-done = bf16[4,48,2048]{2,1,0:T(8,128)(2,1)S(1)} async-done(((bf16[4,48,2048]{2,1,0:T(8,128)(2,1)}), bf16[4,48,2048]{2,1,0:T(8,128)(2,1)S(1)}, u32[]{:S(2)}, u32[]{:S(2)}) %all-to-all-start) | async-done | bytes 786464 | tf_op jit(solution)/shard_map/all_to_all | solution.py:61
  51.7 0.9 copy-done.1
  52.6 3.5 %all-to-all-start.3 = ((bf16[4,48,2048]{2,1,0:T(8,128)(2,1)}), bf16[4,48,2048]{2,1,0:T(8,128)(2,1)S(1)}, u32[]{:S(2)}, u32[]{:S(2)}) async-start(bf16[4,48,2048]{2,1,0:T(8,128)(2,1)} %bitcast.10), calls=%async_computation.3 | async-start | bytes 1572864 | tf_op jit(solution)/shard_map/all_to_all | solution.py:60
  56.1 2.9 %copy.84 = bf16[4,48,2048]{1,0,2:T(4,128)(2,1)S(1)} copy(bf16[4,48,2048]{2,1,0:T(8,128)(2,1)} %copy-done.1) | data formatting | bytes 1572864 | tf_op jit(solution)/shard_map/all_to_all | solution.py:61
  59.0 4.0 %reshape.98 = bf16[8,2,24576]{2,1,0:T(2,128)(2,1)} reshape(bf16[2048,4,48]{2,1,0:T(4,128)(2,1)S(1)} %bitcast.76) | data formatting | bytes 1572864
  63.0 12.9 %all-to-all-done.3 = bf16[4,48,2048]{2,1,0:T(8,128)(2,1)S(1)} async-done(((bf16[4,48,2048]{2,1,0:T(8,128)(2,1)}), bf16[4,48,2048]{2,1,0:T(8,128)(2,1)S(1)}, u32[]{:S(2)}, u32[]{:S(2)}) %all-to-all-start.3) | async-done | bytes 786464 | tf_op jit(solution)/shard_map/all_to_all | solution.py:60
  75.8 4.2 %all-to-all-start.1 = ((bf16[8,2,24576]{2,1,0:T(2,128)(2,1)}), bf16[8,2,24576]{2,1,0:T(2,128)(2,1)}, u32[]{:S(2)}, u32[]{:S(2)}) async-start(bf16[8,2,24576]{2,1,0:T(2,128)(2,1)} %reshape.98), calls=%async_computation.1 | async-start | bytes 1572864 | tf_op jit(solution)/shard_map/all_to_all | solution.py:65
  80.1 1.4 copy.89
  81.5 4.0 %reshape.100 = bf16[8,2,24576]{2,1,0:T(2,128)(2,1)} reshape(bf16[2048,4,48]{2,1,0:T(4,128)(2,1)S(1)} %bitcast.77) | data formatting | bytes 1572864
  85.4 7.3 %all-to-all-done.1 = bf16[8,2,24576]{2,1,0:T(2,128)(2,1)} async-done(((bf16[8,2,24576]{2,1,0:T(2,128)(2,1)}), bf16[8,2,24576]{2,1,0:T(2,128)(2,1)}, u32[]{:S(2)}, u32[]{:S(2)}) %all-to-all-start.1) | async-done | bytes 786464 | tf_op jit(solution)/shard_map/all_to_all | solution.py:65
  92.7 3.5 %all-to-all-start.4 = ((bf16[8,2,24576]{2,1,0:T(2,128)(2,1)}), bf16[8,2,24576]{2,1,0:T(2,128)(2,1)S(1)}, u32[]{:S(2)}, u32[]{:S(2)}) async-start(bf16[8,2,24576]{2,1,0:T(2,128)(2,1)} %reshape.100), calls=%async_computation.4 | async-start | bytes 1572864 | tf_op jit(solution)/shard_map/all_to_all | solution.py:64
  96.3 5.7 %reshape.99 = bf16[2048,4,48]{2,1,0:T(4,128)(2,1)S(1)} reshape(bf16[8,2,24576]{2,1,0:T(2,128)(2,1)} %all-to-all-done.1) | data formatting | bytes 1572864
  102.0 2.2 copy.103
  104.1 8.9 %all-to-all-done.4 = bf16[8,2,24576]{2,1,0:T(2,128)(2,1)S(1)} async-done(((bf16[8,2,24576]{2,1,0:T(2,128)(2,1)}), bf16[8,2,24576]{2,1,0:T(2,128)(2,1)S(1)}, u32[]{:S(2)}, u32[]{:S(2)}) %all-to-all-start.4) | async-done | bytes 786464 | tf_op jit(solution)/shard_map/all_to_all | solution.py:64
  113.0 4.4 %all-to-all-start.2 = ((bf16[8,192,256]{2,1,0:T(8,128)(2,1)}), bf16[8,192,256]{2,1,0:T(8,128)(2,1)}, u32[]{:S(2)}, u32[]{:S(2)}) async-start(bf16[8,192,256]{2,1,0:T(8,128)(2,1)} %bitcast.7), calls=%async_computation.2 | async-start | bytes 1572864 | tf_op jit(solution)/shard_map/all_to_all | solution.py:88
  117.4 2.1 reshape.101
  119.5 2.1 copy.90
  121.7 8.2 %all-to-all-done.2 = bf16[8,192,256]{2,1,0:T(8,128)(2,1)} async-done(((bf16[8,192,256]{2,1,0:T(8,128)(2,1)}), bf16[8,192,256]{2,1,0:T(8,128)(2,1)}, u32[]{:S(2)}, u32[]{:S(2)}) %all-to-all-start.2) | async-done | bytes 786464 | tf_op jit(solution)/shard_map/all_to_all | solution.py:88
  129.9 3.5 %all-to-all-start.5 = ((bf16[8,192,256]{2,1,0:T(8,128)(2,1)}), bf16[8,192,256]{2,1,0:T(8,128)(2,1)S(1)}, u32[]{:S(2)}, u32[]{:S(2)}) async-start(bf16[8,192,256]{2,1,0:T(8,128)(2,1)} %bitcast.13), calls=%async_computation.5 | async-start | bytes 1572864 | tf_op jit(solution)/shard_map/all_to_all | solution.py:87
  133.5 3.0 %convert_reduce_fusion.1 = f32[192,768]{1,0:T(8,128)S(1)} fusion(bf16[768,8,256]{0,2,1:T(8,128)(2,1)} %bitcast.95, bf16[8,192,256]{2,1,0:T(8,128)(2,1)} %all-to-all-done.2), kind=kOutput, calls=%fused_computation.2 | convolution fusion | flops 607371264 | bytes 4521984 | tf_op jit(solution)/shard_map/rcd,fcd->crf/dot_general | solution.py:106
  136.5 6.0 %pad_maximum_fusion = bf16[2048,1536]{1,0:T(8,128)(2,1)} fusion(bf16[2048,768]{1,0:T(8,128)(2,1)} %bitcast.83, bf16[2048,768]{1,0:T(8,128)(2,1)} %bitcast.82), kind=kLoop, calls=%fused_computation.1 | loop fusion | flops 12582912 | bytes 12582912 | tf_op jit(solution)/shard_map/concatenate | solution.py:95
  142.5 3.5 %all-to-all-done.5 = bf16[8,192,256]{2,1,0:T(8,128)(2,1)S(1)} async-done(((bf16[8,192,256]{2,1,0:T(8,128)(2,1)}), bf16[8,192,256]{2,1,0:T(8,128)(2,1)S(1)}, u32[]{:S(2)}, u32[]{:S(2)}) %all-to-all-start.5) | async-done | bytes 786464 | tf_op jit(solution)/shard_map/all_to_all | solution.py:87
  145.9 4.2 %convert_reduce_fusion = f32[192,1536]{1,0:T(8,128)S(1)} fusion(bf16[8,256,1536]{2,1,0:T(8,128)(2,1)} %bitcast.80, bf16[8,192,256]{2,1,0:T(8,128)(2,1)S(1)} %all-to-all-done.5), kind=kOutput, calls=%fused_computation | convolution fusion | flops 1214742528 | bytes 8257536 | tf_op jit(solution)/shard_map/rcd,cdf->crf/dot_general | solution.py:98
  150.2 1.1 multiply_convert_fusion.3
  151.3 0.0 all-gather.9.cloned.1.call-start
  151.3 0.8 pad_maximum_fusion.1
  152.2 1.5 copy.95
  153.7 23.1 %all-gather.11.cloned.1.call-done = bf16[1536,768]{1,0:T(8,128)(2,1)} async-done(((bf16[192,768]{1,0:T(8,128)(2,1)}), bf16[1536,768]{1,0:T(8,128)(2,1)}) %all-gather.11.cloned.1.call-update) | async-done | bytes 2359312 | tf_op jit(solution)/shard_map/all_gather | solution.py:115
  176.8 2.5 fusion.4
  179.3 0.1 reshape.85
  179.4 0.7 reshape.102
  180.1 4.6 %all-to-all-start.8 = ((f32[4,1,384]{2,1,0:T(1,128)}), f32[4,1,384]{2,1,0:T(1,128)S(1)}, u32[]{:S(2)}, u32[]{:S(2)}) async-start(f32[4,1,384]{2,1,0:T(1,128)} %reshape.102), calls=%async_computation.8 | async-start | bytes 12288 | tf_op jit(solution)/shard_map/all_to_all | solution.py:135
  184.7 32.8 %all-gather.9.cloned.1.call-done = bf16[1536,1536]{1,0:T(8,128)(2,1)} async-done(((bf16[192,1536]{1,0:T(8,128)(2,1)}), bf16[1536,1536]{1,0:T(8,128)(2,1)}) %all-gather.9.cloned.1.call-update) | async-done | bytes 4718608 | tf_op jit(solution)/shard_map/all_gather | solution.py:116
  217.5 3.8 %convolution_convert_fusion = bf16[1536,256]{1,0:T(8,128)(2,1)S(1)} fusion(bf16[1536,1536]{1,0:T(8,128)(2,1)} %all-gather.9.cloned.1.call-done, bf16[256,768]{1,0:T(8,128)(2,1)S(1)} %bitcast.88, bf16[256,768]{1,0:T(8,128)(2,1)S(1)} %bitcast.87), kind=kOutput, calls=%fused_computation.4 | convolution fusion | flops 1209925632 | bytes 6291456 | tf_op jit(solution)/shard_map/dot_general | solution.py:81
  221.3 1.0 copy.91
  222.2 4.6 %all-to-all-start.6 = ((bf16[8,4,48,256]{3,2,0,1:T(8,128)(2,1)}), bf16[8,4,48,256]{3,2,0,1:T(8,128)(2,1)S(1)}, u32[]{:S(2)}, u32[]{:S(2)}) async-start(bf16[8,4,48,256]{3,2,0,1:T(8,128)(2,1)} %copy.91), calls=%async_computation.6 | async-start | bytes 1572864 | tf_op jit(solution)/shard_map/all_to_all | solution.py:134
  226.8 0.6 dynamic-slice
  227.4 3.4 %fusion.11 = bf16[1,768,256]{2,1,0:T(8,128)(2,1)} fusion(bf16[1536,768]{1,0:T(8,128)(2,1)} %all-gather.11.cloned.1.call-done, bf16[1536,256]{1,0:T(8,128)(2,1)} %bitcast.26), kind=kOutput, calls=%fused_computation.16 | convolution fusion | flops 604176384 | bytes 3538944 | tf_op jit(solution)/shard_map/dot_general | solution.py:122
  230.8 0.5 broadcast.21
  231.3 0.7 reduce
  232.0 0.1 reshape.103
  232.1 0.1 reshape.96
  232.2 0.5 fusion.26
  232.6 13.1 %all-reduce = f32[8,128]{1,0:T(8,128)S(1)} all-reduce(f32[8,128]{1,0:T(8,128)S(1)} %bitcast.93), channel_id=5, replica_groups=mesh['ctx'=8,'exp'=4] {'ctx'}, use_global_device_ids=true, to_apply=%region_5.6.clone | all-reduce | flops 1024 | bytes 8192
  245.8 1.2 fusion.35
  246.9 0.4 all-to-all-done.6
  247.3 0.1 copy.92
  247.4 1.3 convolution_convert_fusion.3
  248.7 3.5 %all-to-all-start.7 = ((bf16[8,128,256]{2,1,0:T(8,128)(2,1)}), bf16[8,128,256]{2,1,0:T(8,128)(2,1)S(1)}, u32[]{:S(2)}, u32[]{:S(2)}) async-start(bf16[8,128,256]{2,1,0:T(8,128)(2,1)} %convolution_convert_fusion.3), calls=%async_computation.7 | async-start | bytes 1048576 | tf_op jit(solution)/shard_map/all_to_all | solution.py:145
  252.2 3.5 %fusion.12 = bf16[1,256,768]{2,1,0:T(8,128)(2,1)} fusion(bf16[1536,256]{1,0:T(8,128)(2,1)} %bitcast.31, bf16[1536,1536]{1,0:T(8,128)(2,1)} %all-gather.9.cloned.1.call-done), kind=kOutput, calls=%fused_computation.17 | convolution fusion | flops 604176384 | bytes 3538944 | tf_op jit(solution)/shard_map/dot_general | solution.py:78
  255.7 3.5 %fusion.15 = bf16[1,256,768]{2,1,0:T(8,128)(2,1)} fusion(bf16[1536,256]{1,0:T(8,128)(2,1)} %bitcast.31, bf16[1536,1536]{1,0:T(8,128)(2,1)} %all-gather.9.cloned.1.call-done), kind=kOutput, calls=%fused_computation.18 | convolution fusion | flops 604176384 | bytes 3538944 | tf_op jit(solution)/shard_map/dot_general | solution.py:75
  259.2 2.7 %all-to-all-done.7 = bf16[8,128,256]{2,1,0:T(8,128)(2,1)S(1)} async-done(((bf16[8,128,256]{2,1,0:T(8,128)(2,1)}), bf16[8,128,256]{2,1,0:T(8,128)(2,1)S(1)}, u32[]{:S(2)}, u32[]{:S(2)}) %all-to-all-start.7) | async-done | bytes 524320 | tf_op jit(solution)/shard_map/all_to_all | solution.py:145
  261.9 0.3 copy.93
  262.2 1.0 copy.98
  (28 shorter events, 0.4 us)
Async XLA Ops:
  7.2 23.9 %copy-start = (bf16[128,2048]{1,0:T(8,128)(2,1)S(1)}, bf16[128,2048]{1,0:T(8,128)(2,1)}, u32[]{:S(2)}) copy-start(bf16[128,2048]{1,0:T(8,128)(2,1)} %param.7) | copy-start | bytes 1572868
  7.2 126.3 %all-gather.13.cloned.1.call-start = ((), (), s32[]{:S(2)}) async-start(), calls=%async_computation.11 | async-start | bytes 3538944 | tf_op jit(solution)/shard_map/all_gather | solution.py:93
  9.2 127.3 %all-gather.15.cloned.1.call-start = ((), (), s32[]{:S(2)}) async-start(), calls=%async_computation.12 | async-start | bytes 3538944 | tf_op jit(solution)/shard_map/all_gather | solution.py:91
  10.0 126.5 %all-gather.17.cloned.1.call-start = ((), (), s32[]{:S(2)}) async-start(), calls=%async_computation.13 | async-start | bytes 3538944 | tf_op jit(solution)/shard_map/all_gather | solution.py:92
  26.2 25.5 %all-to-all-start = ((bf16[4,48,2048]{2,1,0:T(8,128)(2,1)}), bf16[4,48,2048]{2,1,0:T(8,128)(2,1)S(1)}, u32[]{:S(2)}, u32[]{:S(2)}) async-start(bf16[4,48,2048]{2,1,0:T(8,128)(2,1)} %bitcast.3), calls=%async_computation | async-start | bytes 1572864 | tf_op jit(solution)/shard_map/all_to_all | solution.py:61
  51.7 0.9 copy-start.1
  52.6 23.2 %all-to-all-start.3 = ((bf16[4,48,2048]{2,1,0:T(8,128)(2,1)}), bf16[4,48,2048]{2,1,0:T(8,128)(2,1)S(1)}, u32[]{:S(2)}, u32[]{:S(2)}) async-start(bf16[4,48,2048]{2,1,0:T(8,128)(2,1)} %bitcast.10), calls=%async_computation.3 | async-start | bytes 1572864 | tf_op jit(solution)/shard_map/all_to_all | solution.py:60
  75.8 16.9 %all-to-all-start.1 = ((bf16[8,2,24576]{2,1,0:T(2,128)(2,1)}), bf16[8,2,24576]{2,1,0:T(2,128)(2,1)}, u32[]{:S(2)}, u32[]{:S(2)}) async-start(bf16[8,2,24576]{2,1,0:T(2,128)(2,1)} %reshape.98), calls=%async_computation.1 | async-start | bytes 1572864 | tf_op jit(solution)/shard_map/all_to_all | solution.py:65
  92.7 20.3 %all-to-all-start.4 = ((bf16[8,2,24576]{2,1,0:T(2,128)(2,1)}), bf16[8,2,24576]{2,1,0:T(2,128)(2,1)S(1)}, u32[]{:S(2)}, u32[]{:S(2)}) async-start(bf16[8,2,24576]{2,1,0:T(2,128)(2,1)} %reshape.100), calls=%async_computation.4 | async-start | bytes 1572864 | tf_op jit(solution)/shard_map/all_to_all | solution.py:64
  113.0 16.8 %all-to-all-start.2 = ((bf16[8,192,256]{2,1,0:T(8,128)(2,1)}), bf16[8,192,256]{2,1,0:T(8,128)(2,1)}, u32[]{:S(2)}, u32[]{:S(2)}) async-start(bf16[8,192,256]{2,1,0:T(8,128)(2,1)} %bitcast.7), calls=%async_computation.2 | async-start | bytes 1572864 | tf_op jit(solution)/shard_map/all_to_all | solution.py:88
  129.9 16.1 %all-to-all-start.5 = ((bf16[8,192,256]{2,1,0:T(8,128)(2,1)}), bf16[8,192,256]{2,1,0:T(8,128)(2,1)S(1)}, u32[]{:S(2)}, u32[]{:S(2)}) async-start(bf16[8,192,256]{2,1,0:T(8,128)(2,1)} %bitcast.13), calls=%async_computation.5 | async-start | bytes 1572864 | tf_op jit(solution)/shard_map/all_to_all | solution.py:87
  133.4 43.4 %all-gather.11.cloned.1.call-start = ((), (), s32[]{:S(2)}) async-start(), calls=%async_computation.10 | async-start | bytes 2654208 | tf_op jit(solution)/shard_map/all_gather | solution.py:115
  150.2 26.6 %copy-start.2 = (bf16[1,768,256]{2,1,0:T(8,128)(2,1)S(1)}, bf16[1,768,256]{2,1,0:T(8,128)(2,1)}, u32[]{:S(2)}) copy-start(bf16[1,768,256]{2,1,0:T(8,128)(2,1)} %param.13) | copy-start | bytes 1179652
  151.3 66.2 %all-gather.9.cloned.1.call-start = ((), (), s32[]{:S(2)}) async-start(), calls=%async_computation.9 | async-start | bytes 5308416 | tf_op jit(solution)/shard_map/all_gather | solution.py:116
  152.2 65.3 %copy-start.3 = (bf16[1,256,768]{2,1,0:T(8,128)(2,1)S(1)}, bf16[1,256,768]{2,1,0:T(8,128)(2,1)}, u32[]{:S(2)}) copy-start(bf16[1,256,768]{2,1,0:T(8,128)(2,1)} %param.11) | copy-start | bytes 1179652
  152.2 65.3 %copy-start.4 = (bf16[1,256,768]{2,1,0:T(8,128)(2,1)S(1)}, bf16[1,256,768]{2,1,0:T(8,128)(2,1)}, u32[]{:S(2)}) copy-start(bf16[1,256,768]{2,1,0:T(8,128)(2,1)} %param.12) | copy-start | bytes 1179652
  180.1 42.1 %all-to-all-start.8 = ((f32[4,1,384]{2,1,0:T(1,128)}), f32[4,1,384]{2,1,0:T(1,128)S(1)}, u32[]{:S(2)}, u32[]{:S(2)}) async-start(f32[4,1,384]{2,1,0:T(1,128)} %reshape.102), calls=%async_computation.8 | async-start | bytes 12288 | tf_op jit(solution)/shard_map/all_to_all | solution.py:135
  221.2 5.6 %copy-start.6 = (u32[32]{0:T(128)S(1)}, u32[32]{0:T(128)}, u32[]{:S(2)}) copy-start(u32[32]{0:T(128)} %constant.31) | copy-start | bytes 388
  222.2 25.1 %all-to-all-start.6 = ((bf16[8,4,48,256]{3,2,0,1:T(8,128)(2,1)}), bf16[8,4,48,256]{3,2,0,1:T(8,128)(2,1)S(1)}, u32[]{:S(2)}, u32[]{:S(2)}) async-start(bf16[8,4,48,256]{3,2,0,1:T(8,128)(2,1)} %copy.91), calls=%async_computation.6 | async-start | bytes 1572864 | tf_op jit(solution)/shard_map/all_to_all | solution.py:134
  226.8 18.9 %copy-start.5 = (f32[128,1]{0,1:T(1,128)S(1)}, f32[128,1]{0,1:T(1,128)}, u32[]{:S(2)}) copy-start(f32[128,1]{0,1:T(1,128)} %param.10) | copy-start | bytes 1540
  248.7 13.2 %all-to-all-start.7 = ((bf16[8,128,256]{2,1,0:T(8,128)(2,1)}), bf16[8,128,256]{2,1,0:T(8,128)(2,1)S(1)}, u32[]{:S(2)}, u32[]{:S(2)}) async-start(bf16[8,128,256]{2,1,0:T(8,128)(2,1)} %convolution_convert_fusion.3), calls=%async_computation.7 | async-start | bytes 1048576 | tf_op jit(solution)/shard_map/all_to_all | solution.py:145
Sparse Core Ops, SparseCore 0:
  10.5 35.0 all-gather.12
  47.4 32.3 all-gather.14
  81.7 36.2 all-gather.16
  151.4 25.3 all-gather.10
  178.5 38.9 all-gather.8
where the time goes:
time: 271 us; the launch traced here: 270 us
  waiting for transfers between devices  121 us (45%)
  starting transfers between devices  37 us (14%)
  local copies, waits for them, and re-layouts  33.1 us (12%)
  matrix products  29.3 us (11%)
  blocking collectives  23.4 us (9%)
  between operations  14 us (5%)
  other arithmetic  12.4 us (5%)
    all_gather x1, waiting for transfers between devices, body(): lax.all_gather(grads_own, 'ctx', axis=0, tiled=True)  32.8 us
    all_gather x1, waiting for transfers between devices, body(): lax.all_gather(hidden_own, 'ctx', axis=0, tiled=True)  23.1 us
    unnamed x23, local copies, waits for them, and re-layouts  21 us
    all_to_all x1, waiting for transfers between devices, body(): lax.all_to_all(send_y, 'exp', split_axis=0, concat_axis=0, tiled=True)  19.3 us
    unnamed x1, blocking collectives  13.1 us
    all_to_all x1, waiting for transfers between devices, body(): lax.all_to_all(send_x, 'exp', split_axis=0, concat_axis=0, tiled=True)  12.9 us
    all_gather x1, blocking collectives, body(): all_ids = lax.all_gather(expert_ids, 'ctx', axis=0, tiled=True)  10.3 us
    all_to_all x1, waiting for transfers between devices, body(): lax.all_to_all(group_x, 'ctx', split_axis=2, concat_axis=0, tiled=True)  8.91 us
  transfers between devices with their start and end apart: 14, of which 10 were waited for; matrix products, arithmetic and copies ran while one was open for 24% of the time, Pallas kernels for 0%

commit v1 on v0

--- a/solution.py
+++ b/solution.py
@@ -1,7 +1,13 @@
+import functools
+
 import jax
 import jax.numpy as jnp
 from jax import lax
+from jax.experimental import pallas as pl
+from jax.experimental.pallas import tpu as pltpu
 from jax.sharding import PartitionSpec as P
+
+MESH = pl.DeviceIdType.MESH
 
 
 def slot_table(route_ids, expert_count, capacity):
@@ -160,9 +166,334 @@
     return (token_grads, route_grads, gate_grads, up_grads, down_grads)
 
 
+def ctx_neighbours(me):
+    sib = me + 1 - 2 * (me % 2)
+    across = me + 2 - 4 * ((me // 2) % 2)
+    along = me + 4 - 8 * ((me // 4) % 2)
+    return sib, across, along
+
+
+def enter(ctx_peers, exp_peers):
+    barrier = pltpu.get_barrier_semaphore()
+    for peer in ctx_peers:
+        pl.semaphore_signal(barrier, inc=1, device_id={"ctx": peer}, device_id_type=MESH)
+    for peer in exp_peers:
+        pl.semaphore_signal(barrier, inc=1, device_id={"exp": peer}, device_id_type=MESH)
+    pl.semaphore_wait(barrier, len(ctx_peers) + len(exp_peers))
+
+
+class Gather:
+    def __init__(self, own, out, send_sem, recv_sem, local_sem):
+        me = lax.axis_index("ctx")
+        sib, across, along = ctx_neighbours(me)
+        half = own.shape[0] // 2
+        first, second = pl.ds(0, half), pl.ds(half, half)
+        far = ctx_neighbours(across)[2]
+
+        def copy(k, source, target, peer):
+            return pltpu.make_async_remote_copy(
+                src_ref=source,
+                dst_ref=target,
+                send_sem=send_sem.at[k],
+                recv_sem=recv_sem.at[k],
+                device_id={"ctx": peer},
+                device_id_type=MESH,
+            )
+
+        self.local = pltpu.make_async_copy(own, out.at[me], local_sem)
+        self.c = [
+            copy(0, own.at[first], out.at[me, first], across),
+            copy(1, own.at[second], out.at[me, second], along),
+            copy(2, own.at[second], out.at[me, second], across),
+            copy(3, own.at[first], out.at[me, first], along),
+            copy(4, own, out.at[me], sib),
+            copy(5, out.at[across, first], out.at[across, first], along),
+            copy(6, out.at[along, second], out.at[along, second], across),
+            copy(7, out.at[across], out.at[across], sib),
+            copy(8, out.at[along], out.at[along], sib),
+            copy(9, out.at[far, first], out.at[far, first], sib),
+            copy(10, out.at[far, second], out.at[far, second], sib),
+        ]
+
+    def start_first(self):
+        self.c[0].start()
+        self.c[1].start()
+
+    def start_rest(self):
+        self.c[2].start()
+        self.c[3].start()
+        self.c[4].start()
+        self.local.start()
+
+    def relay(self):
+        self.c[0].wait_recv()
+        self.c[5].start()
+        self.c[1].wait_recv()
+        self.c[6].start()
+
+    def share_near(self):
+        self.c[2].wait_recv()
+        self.c[7].start()
+        self.c[3].wait_recv()
+        self.c[8].start()
+
+    def share_far(self):
+        self.c[5].wait_recv()
+        self.c[9].start()
+        self.c[6].wait_recv()
+        self.c[10].start()
+
+    def finish(self):
+        for k in (4, 7, 8, 9, 10):
+            self.c[k].wait_recv()
+        for one in self.c:
+            one.wait_send()
+        self.local.wait()
+
+
+def dispatch_kernel(
+    n_exp, cap,
+    tok, cot, ids_row, ids_col, weight_col, w_gate, w_up, w_down,
+    x_out, y_out, gate_out, up_out, down_out, table_out,
+    send_x, send_y, g_send, g_recv, g_local, d_send, d_recv, d_local,
+):
+    me_exp = lax.axis_index("exp")
+    me = lax.axis_index("ctx")
+    exp_peers = [lax.rem(me_exp + d, n_exp) for d in range(1, n_exp)]
+    enter(list(ctx_neighbours(me)), exp_peers)
+    gathers = [
+        Gather(own.at[0], out, g_send.at[i], g_recv.at[i], g_local.at[i])
+        for i, (own, out) in enumerate(((w_down, down_out), (w_gate, gate_out), (w_up, up_out)))
+    ]
+    for g in gathers:
+        g.start_first()
+    for g in gathers:
+        g.start_rest()
+    count = tok.shape[0]
+    row = ids_row[...]
+    same = ids_col[...] == row
+    before = lax.broadcasted_iota(jnp.int32, (count, count), 0) < lax.broadcasted_iota(
+        jnp.int32, (count, count), 1
+    )
+    position = jnp.sum(jnp.where(same & before, 1.0, 0.0), axis=0, keepdims=True)
+    target = row * cap + position.astype(jnp.int32)
+    scaled = (weight_col[...] * cot[...].astype(jnp.float32)).astype(jnp.bfloat16)
+    for k in range(n_exp):
+        places = lax.broadcasted_iota(jnp.int32, (cap, count), 0) + k * cap
+        table = jnp.where(places == target, 1.0, 0.0).astype(jnp.bfloat16)
+        table_out[pl.ds(k * cap, cap), :] = table
+        send_x[k] = jnp.dot(table, tok[...], preferred_element_type=jnp.float32).astype(jnp.bfloat16)
+        send_y[k] = jnp.dot(table, scaled, preferred_element_type=jnp.float32).astype(jnp.bfloat16)
+    copies = []
+    for d, peer in enumerate(exp_peers):
+        for which, (source, out) in enumerate(((send_x, x_out), (send_y, y_out))):
+            copies.append(
+                pltpu.make_async_remote_copy(
+                    src_ref=source.at[peer],
+                    dst_ref=out.at[me_exp],
+                    send_sem=d_send.at[d, which],
+                    recv_sem=d_recv.at[d, which],
+                    device_id={"exp": peer},
+                    device_id_type=MESH,
+                )
+            )
+    for one in copies:
+        one.start()
+    kept = [
+        pltpu.make_async_copy(send_x.at[me_exp], x_out.at[me_exp], d_local.at[0]),
+        pltpu.make_async_copy(send_y.at[me_exp], y_out.at[me_exp], d_local.at[1]),
+    ]
+    for one in kept:
+        one.start()
+    for g in gathers:
+        g.relay()
+    for g in gathers:
+        g.share_near()
+    for g in gathers:
+        g.share_far()
+    for one in copies + kept:
+        one.wait()
+    for g in gathers:
+        g.finish()
+
+
+def return_kernel(
+    n_exp, n_ctx,
+    hidden, d_gate, d_up, x_rows, y_rows, back, inner,
+    hidden_out, gate_out, up_out, x_out, y_out, back_out, inner_out,
+    g_send, g_recv, g_local, x_send, x_recv, x_local, d_send, d_recv, d_local,
+):
+    me_exp = lax.axis_index("exp")
+    me = lax.axis_index("ctx")
+    exp_peers = [lax.rem(me_exp + d, n_exp) for d in range(1, n_exp)]
+    ctx_peers = [lax.rem(me + d, n_ctx) for d in range(1, n_ctx)]
+    enter(ctx_peers, exp_peers)
+    gathers = [
+        Gather(own, out, g_send.at[i], g_recv.at[i], g_local.at[i])
+        for i, (own, out) in enumerate(((hidden, hidden_out), (d_gate, gate_out), (d_up, up_out)))
+    ]
+    for g in gathers:
+        g.start_first()
+    copies = []
+    for d, peer in enumerate(exp_peers):
+        for which, (source, out) in enumerate(((back, back_out), (inner, inner_out))):
+            copies.append(
+                pltpu.make_async_remote_copy(
+                    src_ref=source.at[peer],
+                    dst_ref=out.at[me_exp],
+                    send_sem=d_send.at[d, which],
+                    recv_sem=d_recv.at[d, which],
+                    device_id={"exp": peer},
+                    device_id_type=MESH,
+                )
+            )
+    width = x_out.shape[2]
+
+    def columns(at):
+        return pl.ds(pl.multiple_of(at * width, width), width)
+
+    for one in copies:
+        one.start()
+    for g in gathers:
+        g.start_rest()
+    moves = []
+    for d, peer in enumerate(ctx_peers):
+        for which, (source, out) in enumerate(((x_rows, x_out), (y_rows, y_out))):
+            moves.append(
+                pltpu.make_async_remote_copy(
+                    src_ref=source.at[:, columns(peer)],
+                    dst_ref=out.at[me],
+                    send_sem=x_send.at[d, which],
+                    recv_sem=x_recv.at[d, which],
+                    device_id={"ctx": peer},
+                    device_id_type=MESH,
+                )
+            )
+    for one in moves:
+        one.start()
+    kept = [
+        pltpu.make_async_copy(back.at[me_exp], back_out.at[me_exp], d_local.at[0]),
+        pltpu.make_async_copy(inner.at[me_exp], inner_out.at[me_exp], d_local.at[1]),
+        pltpu.make_async_copy(x_rows.at[:, columns(me)], x_out.at[me], x_local.at[0]),
+        pltpu.make_async_copy(y_rows.at[:, columns(me)], y_out.at[me], x_local.at[1]),
+    ]
+    for one in kept:
+        one.start()
+    for g in gathers:
+        g.relay()
+    for g in gathers:
+        g.share_near()
+    for g in gathers:
+        g.share_far()
+    for one in copies + moves + kept:
+        one.wait()
+    for g in gathers:
+        g.finish()
+
+
+def fast_body(tokens, cotangent, expert_ids, route_weights, w_gate, w_up, w_down):
+    n_ctx = lax.axis_size("ctx")
+    n_exp = lax.axis_size("exp")
+    count, width = tokens.shape
+    cap = max(2, (3 * count + 2 * n_exp - 1) // (2 * n_exp))
+    cols = width // n_ctx
+    units = w_gate.shape[2]
+    rows = n_exp * cap
+    bf = jnp.bfloat16
+    vm = pl.BlockSpec(memory_space=pltpu.VMEM)
+    hbm = pl.BlockSpec(memory_space=pl.ANY)
+    dma = pltpu.SemaphoreType.DMA
+    x, y, gate_w, up_w, down_w, table = pl.pallas_call(
+        functools.partial(dispatch_kernel, n_exp, cap),
+        out_shape=(
+            jax.ShapeDtypeStruct((n_exp, cap, width), bf),
+            jax.ShapeDtypeStruct((n_exp, cap, width), bf),
+            jax.ShapeDtypeStruct((n_ctx, cols, units), bf),
+            jax.ShapeDtypeStruct((n_ctx, cols, units), bf),
+            jax.ShapeDtypeStruct((n_ctx, units, cols), bf),
+            jax.ShapeDtypeStruct((rows, count), bf),
+        ),
+        in_specs=[vm] * 5 + [hbm] * 3,
+        out_specs=(hbm,) * 5 + (vm,),
+        scratch_shapes=[
+            pltpu.VMEM((n_exp, cap, width), bf),
+            pltpu.VMEM((n_exp, cap, width), bf),
+            dma((3, 11)), dma((3, 11)), dma((3,)),
+            dma((n_exp - 1, 2)), dma((n_exp - 1, 2)), dma((2,)),
+        ],
+        compiler_params=pltpu.CompilerParams(collective_id=0, has_side_effects=True),
+    )(
+        tokens, cotangent, expert_ids.reshape(1, count), expert_ids.reshape(count, 1),
+        route_weights.reshape(count, 1), w_gate, w_up, w_down,
+    )
+    x = x.reshape(rows, width)
+    y = y.reshape(rows, width)
+    f32 = jnp.float32
+    gate_flat = gate_w.reshape(width, units)
+    up_flat = up_w.reshape(width, units)
+    gate = jnp.dot(x, gate_flat, preferred_element_type=f32)
+    up = jnp.dot(x, up_flat, preferred_element_type=f32)
+    back_sum = jnp.zeros((rows, units), f32)
+    for c in range(n_ctx):
+        back_sum = back_sum + lax.dot_general(
+            y[:, c * cols:(c + 1) * cols], down_w[c], (((1,), (1,)), ((), ())),
+            preferred_element_type=f32,
+        )
+    sig = jax.nn.sigmoid(gate)
+    hidden = (gate * sig * up).astype(bf)
+    d_up = (back_sum * gate * sig).astype(bf)
+    d_gate = (back_sum * up * sig * (1.0 + gate * (1.0 - sig))).astype(bf)
+    inner = jnp.sum(hidden.astype(f32) * back_sum, axis=1)
+    inner = jnp.broadcast_to(
+        jnp.pad(inner.reshape(n_exp, 1, cap), ((0, 0), (0, 0), (0, 128 - cap))), (n_exp, 8, 128)
+    )
+    last = (((1,), (1,)), ((), ()))
+    back = (
+        lax.dot_general(d_gate, gate_flat, last, preferred_element_type=f32)
+        + lax.dot_general(d_up, up_flat, last, preferred_element_type=f32)
+    ).astype(bf).reshape(n_exp, cap, width)
+    hid_all, dg_all, du_all, x_all, y_all, home, home_inner = pl.pallas_call(
+        functools.partial(return_kernel, n_exp, n_ctx),
+        out_shape=(
+            jax.ShapeDtypeStruct((n_ctx, rows, units), bf),
+            jax.ShapeDtypeStruct((n_ctx, rows, units), bf),
+            jax.ShapeDtypeStruct((n_ctx, rows, units), bf),
+            jax.ShapeDtypeStruct((n_ctx, rows, cols), bf),
+            jax.ShapeDtypeStruct((n_ctx, rows, cols), bf),
+            jax.ShapeDtypeStruct((n_exp, cap, width), bf),
+            jax.ShapeDtypeStruct((n_exp, 8, 128), f32),
+        ),
+        in_specs=[hbm] * 7,
+        out_specs=(hbm,) * 7,
+        scratch_shapes=[
+            dma((3, 11)), dma((3, 11)), dma((3,)),
+            dma((n_ctx - 1, 2)), dma((n_ctx - 1, 2)), dma((2,)),
+            dma((n_exp - 1, 2)), dma((n_exp - 1, 2)), dma((2,)),
+        ],
+        compiler_params=pltpu.CompilerParams(collective_id=1, has_side_effects=True),
+    )(hidden, d_gate, d_up, x, y, back, inner)
+    first = (((0,), (0,)), ((), ()))
+    total = n_ctx * rows
+
+    def over_rows(a, b):
+        return lax.dot_general(
+            a.reshape(total, -1), b.reshape(total, -1), first, preferred_element_type=f32
+        ).astype(bf)[None]
+
+    gate_grads = over_rows(x_all, dg_all)
+    up_grads = over_rows(x_all, du_all)
+    down_grads = over_rows(hid_all, y_all)
+    token_grads = lax.dot_general(
+        table, home.reshape(rows, width), first, preferred_element_type=f32
+    ).astype(bf)
+    flat = home_inner[:, 0, :cap].reshape(rows, 1)
+    route = jnp.sum(table.astype(f32) * flat, axis=0).reshape(count, 1)
+    return (token_grads, route / route_weights, gate_grads, up_grads, down_grads)
+
+
 def solution(mesh):
     return jax.shard_map(
-        body,
+        fast_body if mesh.shape["ctx"] == 8 else body,
         mesh=mesh,
         in_specs=(
             P(("ctx", "exp"), None),

time: 271 us -> 129 us (0.48)
  waiting for transfers between devices: 121 us -> 0 us
  Pallas kernels: 0 us -> 102 us
  starting transfers between devices: 37 us -> 0 us
  local copies, waits for them, and re-layouts: 33.1 us -> 6.84 us
  blocking collectives: 23.4 us -> 0 us
  between operations: 14 us -> 0.75 us
  other arithmetic: 12.4 us -> 0.63 us
  matrix products: 29.3 us -> 19.3 us
    pallas_call x0 -> x2, Pallas kernels: none -> 102 us  [the longest x1 52.2 us: fast_body(): pl.pallas_call(functools.partial(return_kernel, n_exp, n_ctx), out_shape=...]
    all_to_all x9 -> x0, waiting for transfers between devices: 63.2 us -> none  [the longest x1 19.3 us: body(): lax.all_to_all(send_y, 'exp', split_axis=0, concat_axis=0, tiled=True)]
    all_gather x5 -> x0, waiting for transfers between devices: 56 us -> none  [the longest x1 32.8 us: body(): lax.all_gather(grads_own, 'ctx', axis=0, tiled=True)]
    all_to_all x9 -> x0, starting transfers between devices: 36.8 us -> none  [the longest x1 4.88 us: body(): lax.all_to_all(send_y, 'exp', split_axis=0, concat_axis=0, tiled=True)]
    unnamed x23 -> x28, local copies, waits for them, and re-layouts: 21 us -> 5.17 us
    unnamed x1 -> x0, blocking collectives: 13.1 us -> none
    all_gather x1 -> x0, blocking collectives: 10.3 us -> none  [body(): all_ids = lax.all_gather(expert_ids, 'ctx', axis=0, tiled=True)]
    dot_general x11 -> x16, matrix products: 29.3 us -> 19.3 us  [the longest x3 6.61 us: over_rows(): lax.dot_general(a.reshape(total, -1), b.reshape(total, -1), first, prefer...]
  transfers between devices with their start and end apart: 14 -> 0, of which waited for: 10 -> 0; matrix products, arithmetic and copies ran while one was open for 24% -> 0% of each run, Pallas kernels for 0% -> 0%
where the time goes in v1:
time: 129 us
  Pallas kernels  102 us (79%)
  matrix products  19.3 us (15%)
  local copies, waits for them, and re-layouts  6.84 us (5%)
    pallas_call x1, Pallas kernels, fast_body(): pl.pallas_call(functools.partial(return_kernel, n_exp, n_ctx), out_shape=...  52.2 us
    pallas_call x1, Pallas kernels, fast_body(): pl.pallas_call(functools.partial(dispatch_kernel, n_exp, cap), out_shape=...  49.5 us
    dot_general x3, matrix products, over_rows(): lax.dot_general(a.reshape(total, -1), b.reshape(total, -1), first, prefer...  6.61 us
    unnamed x28, local copies, waits for them, and re-layouts  5.17 us
    dot_general x8, matrix products, fast_body(): lax.dot_general(y[:, c * cols:(c + 1) * cols], down_w[c], (((1,), (1,)),...  3.34 us
    dot_general x1, matrix products, fast_body(): gate = jnp.dot(x, gate_flat, preferred_element_type=f32)  3.05 us

profile of v1, /device:TPU:0, one launch (start us, length us, event | category | flops | bytes accessed | tf_op | source)
XLA Modules:
  0.0 129.1 jit_solution(22329128077721716)
XLA Ops:
  0.6 1.4 %copy.12.ids_col = s32[128,1]{1,0:T(8,128)} copy(s32[128,1]{0,1:T(1,128)} %param.9) | data formatting | bytes 1024 | tf_op args[2]
  2.0 1.4 %copy.13.weight_col = f32[128,1]{1,0:T(8,128)} copy(f32[128,1]{0,1:T(1,128)} %param.10) | data formatting | bytes 1024 | tf_op args[3]
  3.4 49.5 %shard_map.110 = (bf16[4,48,2048]{2,1,0:T(8,128)(2,1)}, bf16[4,48,2048]{2,1,0:T(8,128)(2,1)}, bf16[8,256,768]{2,1,0:T(8,128)(2,1)}, bf16[8,256,768]{2,1,0:T(8,12...) custom-call(bf16[128,2048]{1,0:T(8,128)(2,1)} %tok.1, bf16[128,2048]{1,0:T(8,128)(2,1)} %cot.1, ...), custom_call_target="tpu_custom_call" | custom-call | tf_op jit(solution)/shard_map/pallas_call | solution.py:406
  52.9 0.0 copy-start
  52.9 0.0 copy-start.2
  52.9 3.1 %fusion.32 = f32[192,768]{1,0:T(8,128)S(1)} fusion(bf16[192,2048]{1,0:T(8,128)(2,1)} %bitcast.81, bf16[2048,768]{1,0:T(8,128)(2,1)} %bitcast.79), kind=kOutput, calls=%fused_computation.53 | convolution fusion | flops 603979776 | bytes 4521984 | tf_op jit(solution)/shard_map/dot_general | solution.py:434
  56.0 0.0 copy-done
  56.0 0.2 copy-done.2
  56.2 0.0 copy-start.3
  56.2 0.0 copy-start.4
  56.2 0.8 fusion.33
  57.0 0.3 copy-done.3
  57.3 1.0 copy-done.4
  58.3 0.3 fusion.14
  58.6 0.3 convolution_add_fusion.7
  58.9 0.3 convolution_add_fusion.6
  59.2 0.3 convolution_add_fusion.5
  59.5 0.3 convolution_add_fusion.4
  59.8 0.3 convolution_add_fusion.3
  60.1 0.0 copy-start.1
  60.1 0.3 convolution_add_fusion.2
  60.4 1.2 multiply_reduce_fusion
  61.7 0.0 copy-start.5
  61.7 0.0 copy-start.6
  61.7 0.4 copy-done.1
  62.1 1.2 fusion.34
  63.3 0.0 copy-start.7
  63.3 2.1 %fusion = bf16[192,2048]{1,0:T(8,128)(2,1)} fusion(f32[192,2048]{1,0:T(8,128)S(1)} %fusion.34, bf16[192,768]{1,0:T(8,128)(2,1)S(1)} %get-tuple-element.34.d_up, bf16[2048,768]{1,0:T(8,128)(2,1)S(1)} %bitcast.78), kind=kOutput, calls=%fused_computation.1 | convolution fusion | flops 604766208 | bytes 5799936 | tf_op jit(solution)/shard_map/dot_general | solution.py:453
  65.3 0.0 copy-done.5
  65.3 0.0 copy-done.6
  65.3 0.0 copy-start.8
  65.4 0.1 reshape.50
  65.4 0.6 broadcast_in_dim.17.inner
  66.1 52.2 %shard_map.111 = (bf16[8,192,768]{2,1,0:T(8,128)(2,1)}, bf16[8,192,768]{2,1,0:T(8,128)(2,1)}, bf16[8,192,768]{2,1,0:T(8,128)(2,1)}, bf16[8,192,256]{2,1,0:T(8,12...) custom-call(bf16[192,768]{1,0:T(8,128)(2,1)} %get-tuple-element.32.hidden, ...), custom_call_target="tpu_custom_call" | custom-call | tf_op jit(solution)/shard_map/pallas_call | solution.py:455
  118.2 0.0 copy-done.7
  118.2 2.3 %convolution_convert_fusion = bf16[128,2048]{1,0:T(8,128)(2,1)} fusion(bf16[192,128]{1,0:T(8,128)(2,1)S(1)} %copy-done.7, bf16[192,2048]{1,0:T(8,128)(2,1)} %bitcast.94), kind=kOutput, calls=%fused_computation.2 | convolution fusion | flops 100925440 | bytes 1359872 | tf_op jit(solution)/shard_map/dot_general | solution.py:486
  120.5 0.0 copy-start.10
  120.5 0.0 copy-start.12
  120.5 0.9 slice_reduce_fusion
  121.4 0.1 mul.46
  121.5 0.1 multiply_reduce_fusion.1
  121.6 0.0 copy-done.8
  121.6 0.5 bitcast_divide_fusion
  122.1 3.5 %fusion.6 = bf16[1,256,768]{2,1,0:T(8,128)(2,1)} fusion(bf16[8,192,256]{2,1,0:T(8,128)(2,1)} %get-tuple-element.26, bf16[8,192,768]{2,1,0:T(8,128)(2,1)} %get-tuple-element.27), kind=kOutput, calls=%fused_computation.18 | convolution fusion | flops 604176384 | bytes 3538944 | tf_op jit(solution)/shard_map/dot_general | solution.py:479
  125.6 0.0 copy-done.10
  125.6 0.0 copy-done.12
  125.6 0.0 copy-start.9
  125.6 0.0 copy-start.11
  125.6 1.6 %fusion.5 = bf16[1,256,768]{2,1,0:T(8,128)(2,1)} fusion(bf16[8,192,256]{2,1,0:T(8,128)(2,1)S(1)} %copy-done.12, bf16[8,192,768]{2,1,0:T(8,128)(2,1)S(1)} %copy-done.10), kind=kOutput, calls=%fused_computation.17 | convolution fusion | flops 604176384 | bytes 3538944 | tf_op jit(solution)/shard_map/dot_general | solution.py:479
  127.2 0.1 copy-done.9
  127.3 0.3 copy-done.11
  127.6 1.6 %fusion.4 = bf16[1,768,256]{2,1,0:T(8,128)(2,1)} fusion(bf16[8,192,768]{2,1,0:T(8,128)(2,1)S(1)} %copy-done.9, bf16[8,192,256]{2,1,0:T(8,128)(2,1)S(1)} %copy-done.11), kind=kOutput, calls=%fused_computation.16 | convolution fusion | flops 604176384 | bytes 3538944 | tf_op jit(solution)/shard_map/dot_general | solution.py:479
  (1 shorter events, 0.0 us)
Async XLA Ops:
  52.9 3.1 %copy-start = (bf16[8,256,768]{2,1,0:T(8,128)(2,1)S(1)}, bf16[8,256,768]{2,1,0:T(8,128)(2,1)}, u32[]{:S(2)}) copy-start(bf16[8,256,768]{2,1,0:T(8,128)(2,1)} %get-tuple-element.21) | copy-start | bytes 9437188
  52.9 3.3 %copy-start.2 = (bf16[4,48,2048]{2,1,0:T(8,128)(2,1)S(1)}, bf16[4,48,2048]{2,1,0:T(8,128)(2,1)}, u32[]{:S(2)}) copy-start(bf16[4,48,2048]{2,1,0:T(8,128)(2,1)} %get-tuple-element.19) | copy-start | bytes 2359300
  56.2 1.1 copy-start.3
  56.2 2.1 %copy-start.4 = (bf16[8,768,256]{2,1,0:T(8,128)(2,1)S(1)}, bf16[8,768,256]{2,1,0:T(8,128)(2,1)}, u32[]{:S(2)}) copy-start(bf16[8,768,256]{2,1,0:T(8,128)(2,1)} %get-tuple-element.23) | copy-start | bytes 9437188
  60.1 2.0 %copy-start.1 = (bf16[8,256,768]{2,1,0:T(8,128)(2,1)S(1)}, bf16[8,256,768]{2,1,0:T(8,128)(2,1)}, u32[]{:S(2)}) copy-start(bf16[8,256,768]{2,1,0:T(8,128)(2,1)} %get-tuple-element.20) | copy-start | bytes 9437188
  61.7 3.7 %copy-start.5 = (bf16[192,768]{1,0:T(8,128)(2,1)}, bf16[192,768]{1,0:T(8,128)(2,1)S(1)}, u32[]{:S(2)}) copy-start(bf16[192,768]{1,0:T(8,128)(2,1)S(1)} %get-tuple-element.33.d_gate) | copy-start | bytes 884740
  61.7 3.7 %copy-start.6 = (bf16[192,768]{1,0:T(8,128)(2,1)}, bf16[192,768]{1,0:T(8,128)(2,1)S(1)}, u32[]{:S(2)}) copy-start(bf16[192,768]{1,0:T(8,128)(2,1)S(1)} %get-tuple-element.34.d_up) | copy-start | bytes 884740
  63.3 54.9 %copy-start.7 = (bf16[192,128]{1,0:T(8,128)(2,1)S(1)}, bf16[192,128]{1,0:T(8,128)(2,1)}, u32[]{:S(2)}) copy-start(bf16[192,128]{1,0:T(8,128)(2,1)} %get-tuple-element.18) | copy-start | bytes 147460
  65.3 56.2 %copy-start.8 = (f32[128,1]{0,1:T(1,128)S(1)}, f32[128,1]{0,1:T(1,128)}, u32[]{:S(2)}) copy-start(f32[128,1]{0,1:T(1,128)} %param.10) | copy-start | bytes 1540
  120.5 5.1 %copy-start.10 = (bf16[8,192,768]{2,1,0:T(8,128)(2,1)S(1)}, bf16[8,192,768]{2,1,0:T(8,128)(2,1)}, u32[]{:S(2)}) copy-start(bf16[8,192,768]{2,1,0:T(8,128)(2,1)} %get-tuple-element.28) | copy-start | bytes 7077892
  120.5 5.1 %copy-start.12 = (bf16[8,192,256]{2,1,0:T(8,128)(2,1)S(1)}, bf16[8,192,256]{2,1,0:T(8,128)(2,1)}, u32[]{:S(2)}) copy-start(bf16[8,192,256]{2,1,0:T(8,128)(2,1)} %get-tuple-element.26) | copy-start | bytes 2359300
  125.6 1.7 %copy-start.9 = (bf16[8,192,768]{2,1,0:T(8,128)(2,1)S(1)}, bf16[8,192,768]{2,1,0:T(8,128)(2,1)}, u32[]{:S(2)}) copy-start(bf16[8,192,768]{2,1,0:T(8,128)(2,1)} %get-tuple-element.29) | copy-start | bytes 7077892
  125.6 2.0 %copy-start.11 = (bf16[8,192,256]{2,1,0:T(8,128)(2,1)S(1)}, bf16[8,192,256]{2,1,0:T(8,128)(2,1)}, u32[]{:S(2)}) copy-start(bf16[8,192,256]{2,1,0:T(8,128)(2,1)} %get-tuple-element.30) | copy-start | bytes 2359300

commit v2 on v0

--- a/solution.py
+++ b/solution.py
@@ -1,7 +1,13 @@
+import functools
+
 import jax
 import jax.numpy as jnp
 from jax import lax
+from jax.experimental import pallas as pl
+from jax.experimental.pallas import tpu as pltpu
 from jax.sharding import PartitionSpec as P
+
+MESH = pl.DeviceIdType.MESH
 
 
 def slot_table(route_ids, expert_count, capacity):
@@ -160,9 +166,367 @@
     return (token_grads, route_grads, gate_grads, up_grads, down_grads)
 
 
+def ctx_neighbours(me):
+    sib = me + 1 - 2 * (me % 2)
+    across = me + 2 - 4 * ((me // 2) % 2)
+    along = me + 4 - 8 * ((me // 4) % 2)
+    return sib, across, along
+
+
+def enter(ctx_peers, exp_peers):
+    barrier = pltpu.get_barrier_semaphore()
+    for peer in ctx_peers:
+        pl.semaphore_signal(barrier, inc=1, device_id={"ctx": peer}, device_id_type=MESH)
+    for peer in exp_peers:
+        pl.semaphore_signal(barrier, inc=1, device_id={"exp": peer}, device_id_type=MESH)
+    pl.semaphore_wait(barrier, len(ctx_peers) + len(exp_peers))
+
+
+class Gather:
+    def __init__(self, own, out, send_sem, recv_sem):
+        me = lax.axis_index("ctx")
+        sib, across, along = ctx_neighbours(me)
+        half = own.shape[0] // 2
+        first, second = pl.ds(0, half), pl.ds(half, half)
+        far = ctx_neighbours(across)[2]
+
+        def copy(k, source, target, peer):
+            return pltpu.make_async_remote_copy(
+                src_ref=source,
+                dst_ref=target,
+                send_sem=send_sem.at[k],
+                recv_sem=recv_sem.at[k],
+                device_id={"ctx": peer},
+                device_id_type=MESH,
+            )
+
+        self.c = [
+            copy(0, own.at[first], out.at[me, first], across),
+            copy(1, own.at[second], out.at[me, second], along),
+            copy(2, own.at[second], out.at[me, second], across),
+            copy(3, own.at[first], out.at[me, first], along),
+            copy(4, own, out.at[me], sib),
+            copy(5, out.at[across, first], out.at[across, first], along),
+            copy(6, out.at[along, second], out.at[along, second], across),
+            copy(7, out.at[across], out.at[across], sib),
+            copy(8, out.at[along], out.at[along], sib),
+            copy(9, out.at[far, first], out.at[far, first], sib),
+            copy(10, out.at[far, second], out.at[far, second], sib),
+        ]
+
+    def start(self, *which):
+        for k in which:
+            self.c[k].start()
+
+    def arrived(self, *which):
+        for k in which:
+            self.c[k].wait_recv()
+
+    def relay(self):
+        self.arrived(0)
+        self.start(5)
+        self.arrived(1)
+        self.start(6)
+
+    def share_near(self):
+        self.arrived(2)
+        self.start(7)
+        self.arrived(3)
+        self.start(8)
+
+    def share_far(self):
+        self.arrived(5)
+        self.start(9)
+        self.arrived(6)
+        self.start(10)
+
+    def sent(self):
+        for one in self.c:
+            one.wait_send()
+
+
+NT = (((1,), (1,)), ((), ()))
+TN = (((0,), (0,)), ((), ()))
+
+
+def dot(a, b, dims):
+    return lax.dot_general(a, b, dims, preferred_element_type=jnp.float32)
+
+
+def kernel(
+    n_exp, n_ctx, cap,
+    tok, cot, ids_row, weight_row, w_gate, w_up, w_down,
+    token_out, route_out, gate_grad, up_grad, down_grad,
+    send_x, send_y, x_rows, y_rows, gate_w, up_w, down_w, table,
+    gate_acc, up_acc, back_acc, hid_all, dg_all, du_all, x_all, y_all,
+    back, inner, home, home_inner, gg_acc, ug_acc, dn_acc,
+    w_send, w_recv, w_local, d_send, d_recv, d_local,
+    s_send, s_recv, m_send, m_recv, m_local, r_send, r_recv, r_local,
+):
+    me_exp = lax.axis_index("exp")
+    me = lax.axis_index("ctx")
+    bf, f32 = jnp.bfloat16, jnp.float32
+    sib, across, along = ctx_neighbours(me)
+    far = ctx_neighbours(across)[2]
+    exp_peers = [lax.rem(me_exp + d, n_exp) for d in range(1, n_exp)]
+    ctx_peers = [lax.rem(me + d, n_ctx) for d in range(1, n_ctx)]
+    enter(ctx_peers, exp_peers)
+
+    weights = [
+        Gather(own.at[0], out, w_send.at[i], w_recv.at[i])
+        for i, (own, out) in enumerate(((w_gate, gate_w), (w_up, up_w), (w_down, down_w)))
+    ]
+    own_weights = [
+        pltpu.make_async_copy(own.at[0], out.at[me], w_local.at[i])
+        for i, (own, out) in enumerate(((w_gate, gate_w), (w_up, up_w), (w_down, down_w)))
+    ]
+    for g in weights:
+        g.start(0, 1)
+    for g in weights:
+        g.start(2, 3)
+
+    count, width = tok.shape
+    cols = width // n_ctx
+
+    def rows_of(at):
+        return pl.ds(pl.multiple_of(at * cap, cap), cap)
+
+    def columns(at):
+        return pl.ds(pl.multiple_of(at * cols, cols), cols)
+
+    down_i = lax.broadcasted_iota(jnp.int32, (count, count), 0)
+    over_i = lax.broadcasted_iota(jnp.int32, (count, count), 1)
+    row = ids_row[...]
+    diagonal = down_i == over_i
+    row_f = row.astype(f32)
+    col_f = jnp.sum(jnp.where(diagonal, row_f, 0.0), axis=1, keepdims=True)
+    weight_col = jnp.sum(jnp.where(diagonal, weight_row[...], 0.0), axis=1, keepdims=True)
+    position = jnp.sum(
+        jnp.where((col_f == row_f) & (down_i < over_i), 1.0, 0.0), axis=0, keepdims=True
+    )
+    target = row * cap + position.astype(jnp.int32)
+    places = lax.broadcasted_iota(jnp.int32, (n_exp * cap, count), 0)
+    table[...] = jnp.where(places == target, 1.0, 0.0).astype(bf)
+
+    def exchange(source, out, sends, recvs, local, which):
+        moves = [
+            pltpu.make_async_remote_copy(
+                src_ref=source.at[rows_of(peer)],
+                dst_ref=out.at[rows_of(me_exp)],
+                send_sem=sends.at[d, which],
+                recv_sem=recvs.at[d, which],
+                device_id={"exp": peer},
+                device_id_type=MESH,
+            )
+            for d, peer in enumerate(exp_peers)
+        ]
+        moves.append(
+            pltpu.make_async_copy(
+                source.at[rows_of(me_exp)], out.at[rows_of(me_exp)], local.at[which]
+            )
+        )
+        for one in moves:
+            one.start()
+        return moves
+
+    send_x[...] = dot(table[...], tok[...], (((1,), (0,)), ((), ()))).astype(bf)
+    sent_x = exchange(send_x, x_rows, d_send, d_recv, d_local, 0)
+    scaled = (weight_col * cot[...].astype(f32)).astype(bf)
+    send_y[...] = dot(table[...], scaled, (((1,), (0,)), ((), ()))).astype(bf)
+    sent_y = exchange(send_y, y_rows, d_send, d_recv, d_local, 1)
+    for g, one in zip(weights, own_weights):
+        g.start(4)
+        one.start()
+    for g in weights:
+        g.relay()
+    for g in weights:
+        g.share_near()
+
+    def spread(source, out, which):
+        moves = [
+            pltpu.make_async_remote_copy(
+                src_ref=source.at[:, columns(peer)],
+                dst_ref=out.at[me],
+                send_sem=m_send.at[d, which],
+                recv_sem=m_recv.at[d, which],
+                device_id={"ctx": peer},
+                device_id_type=MESH,
+            )
+            for d, peer in enumerate(ctx_peers)
+        ]
+        moves.append(
+            pltpu.make_async_copy(source.at[:, columns(me)], out.at[me], m_local.at[which])
+        )
+        for one in moves:
+            one.start()
+        return moves
+
+    for g in weights:
+        g.share_far()
+    for one in sent_x:
+        one.wait()
+    moved = spread(x_rows, x_all, 0)
+    for one in sent_y:
+        one.wait()
+    moved = moved + spread(y_rows, y_all, 1)
+
+    def forward(c, start):
+        xc = x_rows[:, columns(c)]
+        yc = y_rows[:, columns(c)]
+        parts = (
+            dot(xc, gate_w[c], (((1,), (0,)), ((), ()))),
+            dot(xc, up_w[c], (((1,), (0,)), ((), ()))),
+            dot(yc, down_w[c], NT),
+        )
+        for acc, part in zip((gate_acc, up_acc, back_acc), parts):
+            acc[...] = part if start else acc[...] + part
+
+    for one in own_weights:
+        one.wait()
+    forward(me, True)
+    for g in weights:
+        g.arrived(4)
+    forward(sib, False)
+    forward(across, False)
+    forward(along, False)
+    forward(far, False)
+    for g in weights:
+        g.arrived(7, 8)
+    forward(ctx_neighbours(across)[0], False)
+    forward(ctx_neighbours(along)[0], False)
+    for g in weights:
+        g.arrived(9, 10)
+    forward(ctx_neighbours(far)[0], False)
+
+    gate, up, back_sum = gate_acc[...], up_acc[...], back_acc[...]
+    sig = 1.0 / (1.0 + jnp.exp(-gate))
+    hidden = (gate * sig * up).astype(bf)
+    hid_all[me] = hidden
+    dg_all[me] = (back_sum * up * sig * (1.0 + gate * (1.0 - sig))).astype(bf)
+    du_all[me] = (back_sum * gate * sig).astype(bf)
+    states = [
+        Gather(out.at[me], out, s_send.at[i], s_recv.at[i])
+        for i, out in enumerate((hid_all, dg_all, du_all))
+    ]
+    for g in states:
+        g.start(0, 1)
+    for g in states:
+        g.start(2, 3)
+    for g in states:
+        g.start(4)
+    inner[...] = jnp.broadcast_to(
+        jnp.sum(hidden.astype(f32) * back_sum, axis=1, keepdims=True), inner.shape
+    )
+    sent_inner = exchange(inner, home_inner, r_send, r_recv, r_local, 0)
+    for c in range(n_ctx):
+        back[:, c * cols:(c + 1) * cols] = (
+            dot(dg_all[me], gate_w[c], NT) + dot(du_all[me], up_w[c], NT)
+        ).astype(bf)
+    sent_back = exchange(back, home, r_send, r_recv, r_local, 1)
+    for g in states:
+        g.relay()
+    for g in states:
+        g.share_near()
+    for one in moved:
+        one.wait()
+
+    def fold(c, start):
+        xc, yc = x_all[c], y_all[c]
+        parts = (dot(yc, hid_all[c], TN), dot(xc, dg_all[c], TN), dot(xc, du_all[c], TN))
+        for acc, part in zip((dn_acc, gg_acc, ug_acc), parts):
+            acc[...] = part if start else acc[...] + part
+
+    fold(me, True)
+    for g in states:
+        g.arrived(4)
+    fold(sib, False)
+    for g in states:
+        g.share_far()
+    fold(across, False)
+    fold(along, False)
+    for one in sent_inner + sent_back:
+        one.wait()
+    token_out[...] = dot(table[...], home[...], TN).astype(bf)
+    route_out[...] = (
+        jnp.sum(table[...].astype(f32) * home_inner[...], axis=0, keepdims=True) / weight_row[...]
+    )
+    fold(far, False)
+    for g in states:
+        g.arrived(7, 8)
+    fold(ctx_neighbours(across)[0], False)
+    fold(ctx_neighbours(along)[0], False)
+    for g in states:
+        g.arrived(9, 10)
+    fold(ctx_neighbours(far)[0], False)
+    gate_grad[...] = gg_acc[...].astype(bf)
+    up_grad[...] = ug_acc[...].astype(bf)
+    down_grad[...] = dn_acc[...].T.astype(bf)
+    for g in weights + states:
+        g.sent()
+
+
+def fast_body(tokens, cotangent, expert_ids, route_weights, w_gate, w_up, w_down):
+    n_ctx = lax.axis_size("ctx")
+    n_exp = lax.axis_size("exp")
+    count, width = tokens.shape
+    cap = max(2, (3 * count + 2 * n_exp - 1) // (2 * n_exp))
+    cols = width // n_ctx
+    units = w_gate.shape[2]
+    rows = n_exp * cap
+    bf, f32 = jnp.bfloat16, jnp.float32
+    vm = pl.BlockSpec(memory_space=pltpu.VMEM)
+    hbm = pl.BlockSpec(memory_space=pl.ANY)
+    dma = pltpu.SemaphoreType.DMA
+    token_grads, route, gate_grads, up_grads, down_grads = pl.pallas_call(
+        functools.partial(kernel, n_exp, n_ctx, cap),
+        out_shape=(
+            jax.ShapeDtypeStruct((count, width), bf),
+            jax.ShapeDtypeStruct((1, count), f32),
+            jax.ShapeDtypeStruct((cols, units), bf),
+            jax.ShapeDtypeStruct((cols, units), bf),
+            jax.ShapeDtypeStruct((units, cols), bf),
+        ),
+        in_specs=[vm] * 4 + [hbm] * 3,
+        out_specs=(vm,) * 5,
+        scratch_shapes=[pltpu.VMEM((rows, width), bf)] * 4
+        + [
+            pltpu.VMEM((n_ctx, cols, units), bf),
+            pltpu.VMEM((n_ctx, cols, units), bf),
+            pltpu.VMEM((n_ctx, units, cols), bf),
+            pltpu.VMEM((rows, count), bf),
+        ]
+        + [pltpu.VMEM((rows, units), f32)] * 3
+        + [pltpu.VMEM((n_ctx, rows, units), bf)] * 3
+        + [pltpu.VMEM((n_ctx, rows, cols), bf)] * 2
+        + [
+            pltpu.VMEM((rows, width), bf),
+            pltpu.VMEM((rows, count), f32),
+            pltpu.VMEM((rows, width), bf),
+            pltpu.VMEM((rows, count), f32),
+        ]
+        + [pltpu.VMEM((cols, units), f32)] * 3
+        + [
+            dma((3, 11)), dma((3, 11)), dma((3,)),
+            dma((n_exp - 1, 2)), dma((n_exp - 1, 2)), dma((2,)),
+            dma((3, 11)), dma((3, 11)),
+            dma((n_ctx - 1, 2)), dma((n_ctx - 1, 2)), dma((2,)),
+            dma((n_exp - 1, 2)), dma((n_exp - 1, 2)), dma((2,)),
+        ],
+        compiler_params=pltpu.CompilerParams(
+            collective_id=0, has_side_effects=True, vmem_limit_bytes=56 * 1024 * 1024
+        ),
+    )(
+        tokens, cotangent, expert_ids.reshape(1, count), route_weights.reshape(1, count),
+        w_gate, w_up, w_down,
+    )
+    return (
+        token_grads, route.reshape(count, 1), gate_grads[None], up_grads[None], down_grads[None]
+    )
+
+
 def solution(mesh):
     return jax.shard_map(
-        body,
+        fast_body if mesh.shape["ctx"] == 8 else body,
         mesh=mesh,
         in_specs=(
             P(("ctx", "exp"), None),

time: 271 us -> 106 us (0.39)
  waiting for transfers between devices: 121 us -> 0 us
  Pallas kernels: 0 us -> 99.5 us
  starting transfers between devices: 37 us -> 0 us
  matrix products: 29.3 us -> 0 us
  local copies, waits for them, and re-layouts: 33.1 us -> 5.47 us
  blocking collectives: 23.4 us -> 0 us
  between operations: 14 us -> 0.66 us
  other arithmetic: 12.4 us -> 0 us
    pallas_call x0 -> x1, Pallas kernels: none -> 99.5 us  [fast_body(): pl.pallas_call(functools.partial(kernel, n_exp, n_ctx, cap), out_shape=(j...]
    all_to_all x9 -> x0, waiting for transfers between devices: 63.2 us -> none  [the longest x1 19.3 us: body(): lax.all_to_all(send_y, 'exp', split_axis=0, concat_axis=0, tiled=True)]
    all_gather x5 -> x0, waiting for transfers between devices: 56 us -> none  [the longest x1 32.8 us: body(): lax.all_gather(grads_own, 'ctx', axis=0, tiled=True)]
    all_to_all x9 -> x0, starting transfers between devices: 36.8 us -> none  [the longest x1 4.88 us: body(): lax.all_to_all(send_y, 'exp', split_axis=0, concat_axis=0, tiled=True)]
    dot_general x11 -> x0, matrix products: 29.3 us -> none  [the longest x1 4.24 us: body(): jnp.einsum('rcd,cdf->crf', row_x.reshape(own_rows, ctx_size, col_count),...]
    unnamed x23 -> x13, local copies, waits for them, and re-layouts: 21 us -> 5.47 us
    unnamed x1 -> x0, blocking collectives: 13.1 us -> none
    all_gather x1 -> x0, blocking collectives: 10.3 us -> none  [body(): all_ids = lax.all_gather(expert_ids, 'ctx', axis=0, tiled=True)]
  transfers between devices with their start and end apart: 14 -> 0, of which waited for: 10 -> 0; matrix products, arithmetic and copies ran while one was open for 24% -> 0% of each run, Pallas kernels for 0% -> 0%
where the time goes in v2:
time: 106 us
  Pallas kernels  99.5 us (94%)
  local copies, waits for them, and re-layouts  5.47 us (5%)
    pallas_call x1, Pallas kernels, fast_body(): pl.pallas_call(functools.partial(kernel, n_exp, n_ctx, cap), out_shape=(j...  99.5 us
    unnamed x13, local copies, waits for them, and re-layouts  5.47 us

profile of v2, /device:TPU:0, one launch (start us, length us, event | category | flops | bytes accessed | tf_op | source)
XLA Modules:
  0.0 105.6 jit_solution(9022204440182357128)
XLA Ops:
  0.6 99.5 %shard_map.110 = (bf16[128,2048]{1,0:T(8,128)(2,1)}, f32[1,128]{1,0:T(1,128)}, bf16[256,768]{1,0:T(8,128)(2,1)}, bf16[256,768]{1,0:T(8,128)(2,1)}, bf16[768,256]{1,0:T(8,128)(2,1)}) custom-call(bf16[128,2048]{1,0:T(8,128)(2,1)} %tok.1, bf16[128,2048]{1,0:T(8,128)(2,1)} %cot.1, s32[1,128]{1,0:T(1,128)} %bitcast.9, f32[1,128]{1,0:T(1,128)} %bitcast.10, ...), custom_call_target="tpu_custom_call" | custom-call | tf_op jit(solution)/shard_map/pallas_call | solution.py:480
  100.1 0.0 copy-start.3
  100.2 0.0 copy-start.2
  100.2 1.9 %copy.17 = bf16[128,2048]{1,0:T(8,128)(2,1)} copy(bf16[128,2048]{1,0:T(8,128)(2,1)} %get-tuple-element.20) | data formatting | bytes 1048576
  102.1 0.0 copy-done.3
  102.1 0.5 copy.18
  102.6 0.0 copy-done.2
  102.6 0.0 copy-start.1
  102.6 0.7 copy.19
  103.4 0.4 copy-done.1
  103.7 0.0 copy-start
  103.8 0.7 copy.20
  104.5 0.4 copy-done
  104.9 0.7 copy.21
Async XLA Ops:
  100.1 2.0 %copy-start.3 = (f32[1,128]{1,0:T(1,128)S(1)}, f32[1,128]{1,0:T(1,128)}, u32[]{:S(2)}) copy-start(f32[1,128]{1,0:T(1,128)} %get-tuple-element.11) | copy-start | bytes 1540
  100.2 2.5 %copy-start.2 = (bf16[256,768]{1,0:T(8,128)(2,1)S(1)}, bf16[256,768]{1,0:T(8,128)(2,1)}, u32[]{:S(2)}) copy-start(bf16[256,768]{1,0:T(8,128)(2,1)} %get-tuple-element.12) | copy-start | bytes 1179652
  102.6 1.1 %copy-start.1 = (bf16[256,768]{1,0:T(8,128)(2,1)S(1)}, bf16[256,768]{1,0:T(8,128)(2,1)}, u32[]{:S(2)}) copy-start(bf16[256,768]{1,0:T(8,128)(2,1)} %get-tuple-element.13) | copy-start | bytes 1179652
  103.7 1.1 %copy-start = (bf16[768,256]{1,0:T(8,128)(2,1)S(1)}, bf16[768,256]{1,0:T(8,128)(2,1)}, u32[]{:S(2)}) copy-start(bf16[768,256]{1,0:T(8,128)(2,1)} %get-tuple-element.14) | copy-start | bytes 1179652

commit v3 on v2

--- a/solution.py
+++ b/solution.py
@@ -361,42 +361,47 @@
             one.start()
         return moves
 
-    for g in weights:
-        g.share_far()
     for one in sent_x:
         one.wait()
     moved = spread(x_rows, x_all, 0)
+
+    def forward_x(c, start=False):
+        xc = x_rows[:, columns(c)]
+        for acc, weight in ((gate_acc, gate_w), (up_acc, up_w)):
+            part = dot(xc, weight[c], (((1,), (0,)), ((), ())))
+            acc[...] = part if start else acc[...] + part
+
+    def forward_y(c, start=False):
+        part = dot(y_rows[:, columns(c)], down_w[c], NT)
+        back_acc[...] = part if start else back_acc[...] + part
+
+    near = (sib, across, along, ctx_neighbours(across)[0], ctx_neighbours(along)[0])
+    for one in own_weights:
+        one.wait()
+    forward_x(me, True)
+    for g in weights:
+        g.arrived(4)
+        g.arrived(7, 8)
+    weights[0].share_far()
+    for c in near[:3]:
+        forward_x(c)
+    weights[1].share_far()
+    for c in near[3:]:
+        forward_x(c)
+    weights[2].share_far()
     for one in sent_y:
         one.wait()
     moved = moved + spread(y_rows, y_all, 1)
-
-    def forward(c, start):
-        xc = x_rows[:, columns(c)]
-        yc = y_rows[:, columns(c)]
-        parts = (
-            dot(xc, gate_w[c], (((1,), (0,)), ((), ()))),
-            dot(xc, up_w[c], (((1,), (0,)), ((), ()))),
-            dot(yc, down_w[c], NT),
-        )
-        for acc, part in zip((gate_acc, up_acc, back_acc), parts):
-            acc[...] = part if start else acc[...] + part
-
-    for one in own_weights:
-        one.wait()
-    forward(me, True)
-    for g in weights:
-        g.arrived(4)
-    forward(sib, False)
-    forward(across, False)
-    forward(along, False)
-    forward(far, False)
-    for g in weights:
-        g.arrived(7, 8)
-    forward(ctx_neighbours(across)[0], False)
-    forward(ctx_neighbours(along)[0], False)
+    forward_y(me, True)
+    for c in near:
+        forward_y(c)
+    forward_x(far)
+    forward_y(far)
     for g in weights:
         g.arrived(9, 10)
-    forward(ctx_neighbours(far)[0], False)
+    last = ctx_neighbours(far)[0]
+    forward_x(last)
+    forward_y(last)
 
     gate, up, back_sum = gate_acc[...], up_acc[...], back_acc[...]
     sig = 1.0 / (1.0 + jnp.exp(-gate))
@@ -436,14 +441,19 @@
         for acc, part in zip((dn_acc, gg_acc, ug_acc), parts):
             acc[...] = part if start else acc[...] + part
 
+    for g in states:
+        g.arrived(4)
     fold(me, True)
-    for g in states:
-        g.arrived(4)
     fold(sib, False)
-    for g in states:
-        g.share_far()
+    states[0].share_far()
     fold(across, False)
+    states[1].share_far()
     fold(along, False)
+    for g in states:
+        g.arrived(7, 8)
+    fold(ctx_neighbours(across)[0], False)
+    fold(ctx_neighbours(along)[0], False)
+    states[2].share_far()
     for one in sent_inner + sent_back:
         one.wait()
     token_out[...] = dot(table[...], home[...], TN).astype(bf)
@@ -451,10 +461,6 @@
         jnp.sum(table[...].astype(f32) * home_inner[...], axis=0, keepdims=True) / weight_row[...]
     )
     fold(far, False)
-    for g in states:
-        g.arrived(7, 8)
-    fold(ctx_neighbours(across)[0], False)
-    fold(ctx_neighbours(along)[0], False)
     for g in states:
         g.arrived(9, 10)
     fold(ctx_neighbours(far)[0], False)
@@ -463,6 +469,11 @@
     down_grad[...] = dn_acc[...].T.astype(bf)
     for g in weights + states:
         g.sent()
+
+
+def hand_over(*refs):
+    for source, out in zip(refs[:5], refs[5:]):
+        out[...] = source[...]
 
 
 def fast_body(tokens, cotangent, expert_ids, route_weights, w_gate, w_up, w_down):
@@ -519,6 +530,13 @@
         tokens, cotangent, expert_ids.reshape(1, count), route_weights.reshape(1, count),
         w_gate, w_up, w_down,
     )
+    results = (token_grads, route, gate_grads, up_grads, down_grads)
+    token_grads, route, gate_grads, up_grads, down_grads = pl.pallas_call(
+        hand_over,
+        out_shape=tuple(jax.ShapeDtypeStruct(r.shape, r.dtype) for r in results),
+        in_specs=[vm] * 5,
+        out_specs=(vm,) * 5,
+    )(*results)
     return (
         token_grads, route.reshape(count, 1), gate_grads[None], up_grads[None], down_grads[None]
     )

time: 106 us -> 99.8 us (0.942)
  local copies, waits for them, and re-layouts: 5.47 us -> 0 us
    unnamed x13 -> x0, local copies, waits for them, and re-layouts: 5.47 us -> none
    pallas_call x1, Pallas kernels: 99.5 us -> 96 us  [fast_body(): pl.pallas_call(functools.partial(kernel, n_exp, n_ctx, cap), out_shape=(j...]
    pallas_call x0 -> x1, Pallas kernels: none -> 2.6 us  [fast_body(): pl.pallas_call(hand_over, out_shape=tuple((jax.ShapeDtypeStruct(r.shape,...]
where the time goes in v3:
time: 99.8 us; the launch traced here: 99.2 us
  Pallas kernels  98.6 us (99%)
    pallas_call x1, Pallas kernels, fast_body(): pl.pallas_call(functools.partial(kernel, n_exp, n_ctx, cap), out_shape=(j...  96 us
    pallas_call x1, Pallas kernels, fast_body(): pl.pallas_call(hand_over, out_shape=tuple((jax.ShapeDtypeStruct(r.shape,...  2.6 us

profile of v3, /device:TPU:0, one launch (start us, length us, event | category | flops | bytes accessed | tf_op | source)
XLA Modules:
  0.0 99.2 jit_solution(7435876222543572468)
XLA Ops:
  0.6 96.0 %shard_map.110 = (bf16[128,2048]{1,0:T(8,128)(2,1)}, f32[1,128]{1,0:T(1,128)}, bf16[256,768]{1,0:T(8,128)(2,1)}, bf16[256,768]{1,0:T(8,128)(2,1)}, bf16[768,256]{1,0:T(8,128)(2,1)}) custom-call(bf16[128,2048]{1,0:T(8,128)(2,1)} %tok.1, bf16[128,2048]{1,0:T(8,128)(2,1)} %cot.1, s32[1,128]{1,0:T(1,128)} %bitcast.6, f32[1,128]{1,0:T(1,128)} %bitcast.7, ...), custom_call_target="tpu_custom_call" | custom-call | tf_op jit(solution)/shard_map/pallas_call | solution.py:491
  96.6 2.6 %shard_map.111 = (bf16[128,2048]{1,0:T(8,128)(2,1)}, f32[1,128]{1,0:T(1,128)}, bf16[256,768]{1,0:T(8,128)(2,1)}, bf16[256,768]{1,0:T(8,128)(2,1)}, bf16[768,256]{1,0:T(8,128)(2,1)}) custom-call(bf16[128,2048]{1,0:T(8,128)(2,1)} %get-tuple-element.15.refs_0_, f32[1,128]{1,0:T(1,128)} %get-tuple-element.16.refs_1_, ...), custom_call_target="tpu_custom_call" | custom-call | tf_op jit(solution)/shard_map/pallas_call | solution.py:534

commit v4 on v3

--- a/solution.py
+++ b/solution.py
@@ -255,13 +255,14 @@
 
 def kernel(
     n_exp, n_ctx, cap,
-    tok, cot, ids_row, weight_row, w_gate, w_up, w_down,
+    tok_in, cot_in, ids_row, weight_row, w_gate, w_up, w_down,
     token_out, route_out, gate_grad, up_grad, down_grad,
     send_x, send_y, x_rows, y_rows, gate_w, up_w, down_w, table,
     gate_acc, up_acc, back_acc, hid_all, dg_all, du_all, x_all, y_all,
     back, inner, home, home_inner, gg_acc, ug_acc, dn_acc,
     w_send, w_recv, w_local, d_send, d_recv, d_local,
     s_send, s_recv, m_send, m_recv, m_local, r_send, r_recv, r_local,
+    tok, cot, in_sem,
 ):
     me_exp = lax.axis_index("exp")
     me = lax.axis_index("ctx")
@@ -270,6 +271,12 @@
     far = ctx_neighbours(across)[2]
     exp_peers = [lax.rem(me_exp + d, n_exp) for d in range(1, n_exp)]
     ctx_peers = [lax.rem(me + d, n_ctx) for d in range(1, n_ctx)]
+    loads = [
+        pltpu.make_async_copy(tok_in, tok, in_sem.at[0]),
+        pltpu.make_async_copy(cot_in, cot, in_sem.at[1]),
+    ]
+    for one in loads:
+        one.start()
     enter(ctx_peers, exp_peers)
 
     weights = [
@@ -329,8 +336,10 @@
             one.start()
         return moves
 
+    loads[0].wait()
     send_x[...] = dot(table[...], tok[...], (((1,), (0,)), ((), ()))).astype(bf)
     sent_x = exchange(send_x, x_rows, d_send, d_recv, d_local, 0)
+    loads[1].wait()
     scaled = (weight_col * cot[...].astype(f32)).astype(bf)
     send_y[...] = dot(table[...], scaled, (((1,), (0,)), ((), ()))).astype(bf)
     sent_y = exchange(send_y, y_rows, d_send, d_recv, d_local, 1)
@@ -406,15 +415,16 @@
     gate, up, back_sum = gate_acc[...], up_acc[...], back_acc[...]
     sig = 1.0 / (1.0 + jnp.exp(-gate))
     hidden = (gate * sig * up).astype(bf)
-    hid_all[me] = hidden
-    dg_all[me] = (back_sum * up * sig * (1.0 + gate * (1.0 - sig))).astype(bf)
-    du_all[me] = (back_sum * gate * sig).astype(bf)
     states = [
         Gather(out.at[me], out, s_send.at[i], s_recv.at[i])
         for i, out in enumerate((hid_all, dg_all, du_all))
     ]
-    for g in states:
-        g.start(0, 1)
+    hid_all[me] = hidden
+    states[0].start(0, 1)
+    dg_all[me] = (back_sum * up * sig * (1.0 + gate * (1.0 - sig))).astype(bf)
+    states[1].start(0, 1)
+    du_all[me] = (back_sum * gate * sig).astype(bf)
+    states[2].start(0, 1)
     for g in states:
         g.start(2, 3)
     for g in states:
@@ -497,7 +507,7 @@
             jax.ShapeDtypeStruct((cols, units), bf),
             jax.ShapeDtypeStruct((units, cols), bf),
         ),
-        in_specs=[vm] * 4 + [hbm] * 3,
+        in_specs=[hbm] * 2 + [vm] * 2 + [hbm] * 3,
         out_specs=(vm,) * 5,
         scratch_shapes=[pltpu.VMEM((rows, width), bf)] * 4
         + [
@@ -522,6 +532,7 @@
             dma((3, 11)), dma((3, 11)),
             dma((n_ctx - 1, 2)), dma((n_ctx - 1, 2)), dma((2,)),
             dma((n_exp - 1, 2)), dma((n_exp - 1, 2)), dma((2,)),
+            pltpu.VMEM((count, width), bf), pltpu.VMEM((count, width), bf), dma((2,)),
         ],
         compiler_params=pltpu.CompilerParams(
             collective_id=0, has_side_effects=True, vmem_limit_bytes=56 * 1024 * 1024

time: 99.8 us -> 99.3 us (level)
  no operation moved by 1% of the time
where the time goes in v4:
time: 99.3 us; the launch traced here: 98.7 us
  Pallas kernels  98.1 us (99%)
    pallas_call x1, Pallas kernels, fast_body(): pl.pallas_call(functools.partial(kernel, n_exp, n_ctx, cap), out_shape=(j...  95.5 us
    pallas_call x1, Pallas kernels, fast_body(): pl.pallas_call(hand_over, out_shape=tuple((jax.ShapeDtypeStruct(r.shape,...  2.6 us

profile of v4, /device:TPU:0, one launch (start us, length us, event | category | flops | bytes accessed | tf_op | source)
XLA Modules:
  0.0 98.7 jit_solution(6983181699835364588)
XLA Ops:
  0.6 95.5 %shard_map.110 = (bf16[128,2048]{1,0:T(8,128)(2,1)}, f32[1,128]{1,0:T(1,128)}, bf16[256,768]{1,0:T(8,128)(2,1)}, bf16[256,768]{1,0:T(8,128)(2,1)}, bf16[768,256]{1,0:T(8,128)(2,1)}) custom-call(bf16[128,2048]{1,0:T(8,128)(2,1)} %tok_in.1, bf16[128,2048]{1,0:T(8,128)(2,1)} %cot_in.1, s32[1,128]{1,0:T(1,128)} %bitcast.6, f32[1,128]{1,0:T(1,128)} %bitcast.7, ...), custom_call_target="tpu_custom_call" | custom-call | tf_op jit(solution)/shard_map/pallas_call | solution.py:501
  96.1 2.6 %shard_map.111 = (bf16[128,2048]{1,0:T(8,128)(2,1)}, f32[1,128]{1,0:T(1,128)}, bf16[256,768]{1,0:T(8,128)(2,1)}, bf16[256,768]{1,0:T(8,128)(2,1)}, bf16[768,256]{1,0:T(8,128)(2,1)}) custom-call(bf16[128,2048]{1,0:T(8,128)(2,1)} %get-tuple-element.15.refs_0_, f32[1,128]{1,0:T(1,128)} %get-tuple-element.16.refs_1_, ...), custom_call_target="tpu_custom_call" | custom-call | tf_op jit(solution)/shard_map/pallas_call | solution.py:545
